TPU v7x, 128 devices: a whole 4x4x4 slice. The times are simulated.
128 devices in a mesh: tile: 16 (over x, z_lo, core), col: 8 (over y, z_hi).
Axes of the slice: x: 4, y: 4, z: 4 (z_hi: 2, z_lo: 2; z = z_hi * 2 + z_lo), core: 2. Of those that a mesh axis runs over, the one named last changes fastest.
Arguments:
- u_velocity: float32 [8192, 4096], P('tile', 'col'), may hold values from -12 to 12
- v_velocity: float32 [8192, 4096], P('tile', 'col'), may hold values from -12 to 12
- ocean_mask: int32 [64, 32], P('tile', 'col'), may hold values from 0 to 1, as said below
- tile_owner: int32 [64, 32], P('tile', 'col'), may hold values from 0 to 15, as said below
- lower_edge_quarter_turns: int32 [16], replicated, may hold values from 0 to 3
Outputs:
- library: float32 [16, 8, 16, 16, 1024], P('tile', 'col')
- gram: float32 [16, 16], replicated
Inputs may be any that keep to these rules, and one draw needn't show every extreme that they name: `ocean_mask`: in every column of devices (4 x 4 tile blocks), at least one device has only ocean tiles. `tile_owner`: among the ocean tiles of one device at most 1 share an owner; the ocean tiles of one column of devices are spread over its 16 owners so that the owners' counts differ by at most one. Land tiles carry an owner that is not used.
All inputs are finite; a program needn't handle non-finite values.
Results may differ from a plain program's by a relative error of at most 0.00014.
Values sent between devices are 32-bit elements; how exact they have to be, the bound alone decides.
No kernel may reach another device: no remote copies, remote signals or barrier semaphores. Data moves between devices by JAX's collectives and lax.ppermute only.
A program may use at most 192 MiB of HBM per device.

v0:
```python
import jax
import jax.numpy as jnp
from jax import lax
from jax.sharding import PartitionSpec as P

PASSES = 8
KAPPA = 0.2


def with_halo(cells, sides, width):
    for axis, dim in sides:
        count = lax.axis_size(axis)
        head = lax.slice_in_dim(cells, 0, width, axis=dim)
        tail = lax.slice_in_dim(cells, cells.shape[dim] - width, cells.shape[dim], axis=dim)
        cells = jnp.concatenate(
            [
                lax.ppermute(tail, axis, [(i, (i + 1) % count) for i in range(count)]),
                cells,
                lax.ppermute(head, axis, [((i + 1) % count, i) for i in range(count)]),
            ],
            axis=dim,
        )
    return cells


def quarter(first, second, turns):
    cosine = jnp.where(turns == 0, 1.0, jnp.where(turns == 2, -1.0, 0.0)).astype(first.dtype)
    sine = jnp.where(turns == 1, 1.0, jnp.where(turns == 3, -1.0, 0.0)).astype(first.dtype)
    return (cosine * first - sine * second, sine * first + cosine * second)


def turn_rims(padded, width, k_top, k_bottom):
    top_u, top_v = quarter(padded[0, :width], padded[1, :width], k_top)
    low_u, low_v = quarter(padded[0, -width:], padded[1, -width:], k_bottom)
    upper = jnp.stack([top_u, top_v])
    lower = jnp.stack([low_u, low_v])
    return jnp.concatenate([upper, padded[:, width:-width], lower], axis=1)


def relax(padded):
    centre = padded[:, 1:-1, 1:-1]
    beside_all = (
        padded[:, :-2, 1:-1] + padded[:, 2:, 1:-1] + padded[:, 1:-1, :-2] + padded[:, 1:-1, 2:]
    )
    return centre + KAPPA * (beside_all - 4.0 * centre)


def derive(padded):
    first = padded[..., 0, :, :]
    second = padded[..., 1, :, :]
    u_part = first[..., 1:-1, 1:-1]
    v_part = second[..., 1:-1, 1:-1]
    u_dx = (first[..., 1:-1, 2:] - first[..., 1:-1, :-2]) * 0.5
    u_dy = (first[..., 2:, 1:-1] - first[..., :-2, 1:-1]) * 0.5
    v_dx = (second[..., 1:-1, 2:] - second[..., 1:-1, :-2]) * 0.5
    v_dy = (second[..., 2:, 1:-1] - second[..., :-2, 1:-1]) * 0.5
    return jnp.stack([u_part, v_part, v_dx - u_dy, u_dy + v_dx, u_dx - v_dy], axis=-3)


def make_terms(base):
    u_part = base[..., 0, :]
    v_part = base[..., 1, :]
    vort = base[..., 2, :]
    strain = base[..., 3, :]
    stretch = base[..., 4, :]
    listed = [
        u_part,
        v_part,
        vort,
        strain,
        stretch,
        vort * vort,
        vort * strain,
        vort * stretch,
        strain * strain,
        stretch * stretch,
        strain * stretch,
        u_part * vort,
        v_part * vort,
        u_part * strain,
        v_part * stretch,
        u_part * v_part,
    ]
    return jnp.stack(listed, axis=-2)


def to_tiles(field, grid_x, grid_y, side):
    leading = field.shape[:-2]
    shaped = field.reshape(leading + (grid_x, side, grid_y, side))
    shaped = jnp.swapaxes(shaped, -3, -2)
    return shaped.reshape(leading + (grid_x * grid_y, side * side))


def per_device(u_velocity, v_velocity, ocean_mask, tile_owner, lower_edge_quarter_turns):
    rows_tile = lax.axis_size("tile")
    here = lax.axis_index("tile")
    k_top = lower_edge_quarter_turns[here]
    k_bottom = (4 - lower_edge_quarter_turns[(here + 1) % rows_tile]) % 4
    field = jnp.stack([u_velocity, v_velocity])
    for step in range(PASSES):
        padded = with_halo(field, (("tile", 1), ("col", 2)), 1)
        field = relax(turn_rims(padded, 1, k_top, k_bottom))
    fine_rows, fine_cols = u_velocity.shape
    coarse = field.reshape(2, fine_rows // 4, 4, fine_cols // 4, 4).mean(axis=(2, 4))
    coarse_pad = with_halo(coarse, (("tile", 1), ("col", 2)), 1)
    coarse_pad = turn_rims(coarse_pad, 1, k_top, k_bottom)
    grid_x, grid_y = ocean_mask.shape
    side = coarse.shape[1] // grid_x
    starting_tile_set = jnp.swapaxes(to_tiles(derive(coarse_pad), grid_x, grid_y, side), 0, 1)
    live = ocean_mask.reshape(-1) == 1
    owners = tile_owner.reshape(-1)
    tiles = live.shape[0]
    slots = tiles // rows_tile
    local = jnp.arange(tiles, dtype=jnp.int32)
    same = (owners[:, None] == owners[None, :]) & live[None, :] & (local[None, :] < local[:, None])
    slot = jnp.sum(same.astype(jnp.int32), axis=1)
    target = jnp.arange(rows_tile * slots, dtype=jnp.int32)
    chosen_terms = (
        live[None, :]
        & (owners[None, :] == target[:, None] // slots)
        & (slot[None, :] == target[:, None] % slots)
    ).astype(jnp.float32)
    library = make_terms(
        lax.all_to_all(
            jnp.einsum(
                "vh,hsd->vsd", chosen_terms, starting_tile_set, precision=lax.Precision.HIGHEST
            ),
            "tile",
            split_axis=0,
            concat_axis=0,
            tiled=True,
        )
    )
    part = jnp.einsum("pnc,pmc->nm", library, library, precision=lax.Precision.HIGHEST)
    gram = lax.psum(part, ("tile", "col")) / (fine_rows // 4 * (fine_cols // 4))
    return (library[None, None], gram)


def solution(mesh):
    in_specs = (P("tile", "col"), P("tile", "col"), P("tile", "col"), P("tile", "col"), P())
    out_specs = (P("tile", "col", None, None, None), P())
    return jax.shard_map(
        per_device, mesh=mesh, in_specs=in_specs, out_specs=out_specs, check_vma=False
    )
```

profile of v0, /device:TPU:1, one launch (start us, length us, event | category | flops | bytes accessed | tf_op | source)
XLA Modules:
  0.0 374.1 jit_solution(4603771623657914441)
XLA Ops:
  1.6 3.1 collective-permute-start
  8.2 3.5 collective-permute-start.2
  12.0 2.5 collective-permute-start.3
  21.4 6.4 %fusion.45 = f32[2,512,512]{2,1,0:T(8,128)S(1)} fusion(f32[2,514,1]{2,1,0:T(8,128)} %copy-done.15, f32[2,1,512]{2,1,0:T(1,128)S(1)} %collective-permute-done.1, f32[2,1,512]{2,1,0:T(1,128)S(1)} %collective-permute-done, f32[1,512,512]{2,1,0:T(8,128)S(1)} %bitcast.34, f32[1,512,512]{2,1,0:T(8,128)S(1)} %bitcast.28, f32[2,514,1]{2,1,0:T(8,128)} %copy-done.13, ...), kind=kLoop, calls=%fused_computation.129 | loop fusion | flops 10485760 | bytes 6324288 | tf_op jit(solution)/shard_map/add | solution.py:45
  34.3 4.6 %collective-permute-start.7 = (f32[2,514,1]{1,0,2:T(2,128)S(1)}, f32[2,514,1]{1,0,2:T(2,128)S(1)}, u32[]{:S(2)}, u32[]{:S(2)}) collective-permute-start(f32[2,514,1]{1,0,2:T(2,128)S(1)} %copy.209), channel_id=1, source_target_pairs={{1,0},{2,1},{3,2},{4,3},{5,4},{6,5},{7,6},{0,7},{9,8},{10,9},{11,1... | collective-permute-start | bytes 12344 | tf_op jit(solution)/shard_map/ppermute | solution.py:19
  44.0 8.1 %fusion.39 = f32[2,512,512]{2,1,0:T(8,128)S(1)} fusion(f32[2,512,512]{2,1,0:T(8,128)} %copy-done.9, f32[2,514,1]{2,1,0:T(8,128)S(1)} %copy-done.16, f32[2,1,512]{2,1,0:T(1,128)S(1)} %collective-permute-done.5, f32[2,1,512]{2,1,0:T(1,128)S(1)} %collective-permute-done.4, f32[2,514,1]{2,1,0:T(8,128)} %copy-done.14, f32[2,512,514]{2,1,0:T(8,128)S(1)} %slice.600, ...), kind=kLoop, calls=%fused_computation.113 | loop fusion | flops 8912896 | bytes 6324288 | tf_op jit(solution)/shard_map/add | solution.py:45
  53.3 3.0 collective-permute-start.9
  59.6 3.8 %collective-permute-start.11 = (f32[2,514,1]{1,0,2:T(2,128)S(1)}, f32[2,514,1]{1,0,2:T(2,128)S(1)}, u32[]{:S(2)}, u32[]{:S(2)}) collective-permute-start(f32[2,514,1]{1,0,2:T(2,128)S(1)} %copy.215), channel_id=1, source_target_pairs={{1,0},{2,1},{3,2},{4,3},{5,4},{6,5},{7,6},{0,7},{9,8},{10,9},{11,1... | collective-permute-start | bytes 12344 | tf_op jit(solution)/shard_map/ppermute | solution.py:19
  66.1 5.0 %fusion.33 = f32[2,512,512]{2,1,0:T(8,128)S(1)} fusion(f32[2,512,512]{2,1,0:T(8,128)S(1)} %fusion.39, f32[2,514,1]{2,1,0:T(8,128)S(1)} %copy.217, f32[2,1,512]{2,1,0:T(1,128)S(1)} %collective-permute-done.9, f32[2,1,512]{2,1,0:T(1,128)S(1)} %collective-permute-done.8, f32[2,514,1]{2,1,0:T(8,128)S(1)} %copy.216, f32[2,512,514]{2,1,0:T(8,128)S(1)} %slice.603, ...), kind=kLoop, calls=%fused_computation.97 | loop fusion | flops 8912896 | bytes 6324288 | tf_op jit(solution)/shard_map/add | solution.py:45
  71.8 4.6 %collective-permute-start.13 = (f32[2,1,512]{2,1,0:T(1,128)S(1)}, f32[2,1,512]{2,1,0:T(1,128)S(1)}, u32[]{:S(2)}, u32[]{:S(2)}) collective-permute-start(f32[2,1,512]{2,1,0:T(1,128)S(1)} %get-tuple-element.85), channel_id=1, source_target_pairs={{8,0},{16,8},{24,16},{32,24},{40,32},{48,40},{56,48},{64,56},{72,6... | collective-permute-start | bytes 12296 | tf_op jit(solution)/shard_map/ppermute | solution.py:19
  79.9 3.6 collective-permute-start.15
  86.0 5.0 %fusion.27 = f32[2,512,512]{2,1,0:T(8,128)S(1)} fusion(f32[2,512,512]{2,1,0:T(8,128)S(1)} %copy-done.1, f32[2,514,1]{2,1,0:T(8,128)S(1)} %copy.223, f32[2,1,512]{2,1,0:T(1,128)S(1)} %collective-permute-done.13, f32[2,1,512]{2,1,0:T(1,128)S(1)} %collective-permute-done.12, f32[2,514,1]{2,1,0:T(8,128)S(1)} %copy.222, f32[2,512,514]{2,1,0:T(8,128)S(1)} %slice.606, ...), kind=kLoop, calls=%fused_computation.81 | loop fusion | flops 8912896 | bytes 6324288 | tf_op jit(solution)/shard_map/add | solution.py:45
  91.0 5.6 %collective-permute-start.17 = (f32[2,1,512]{2,1,0:T(1,128)S(1)}, f32[2,1,512]{2,1,0:T(1,128)S(1)}, u32[]{:S(2)}, u32[]{:S(2)}) collective-permute-start(f32[2,1,512]{2,1,0:T(1,128)S(1)} %get-tuple-element.83), channel_id=1, source_target_pairs={{8,0},{16,8},{24,16},{32,24},{40,32},{48,40},{56,48},{64,56},{72,6... | collective-permute-start | bytes 12296 | tf_op jit(solution)/shard_map/ppermute | solution.py:19
  97.9 2.7 collective-permute-start.18
  100.8 2.7 collective-permute-start.19
  106.4 5.0 %fusion.21 = f32[2,512,512]{2,1,0:T(8,128)S(1)} fusion(f32[2,512,512]{2,1,0:T(8,128)S(1)} %copy-done.3, f32[2,514,1]{2,1,0:T(8,128)S(1)} %copy.229, f32[2,1,512]{2,1,0:T(1,128)S(1)} %collective-permute-done.17, f32[2,1,512]{2,1,0:T(1,128)S(1)} %collective-permute-done.16, f32[2,514,1]{2,1,0:T(8,128)S(1)} %copy.228, f32[2,512,514]{2,1,0:T(8,128)S(1)} %slice.609, ...), kind=kLoop, calls=%fused_computation.65 | loop fusion | flops 8912896 | bytes 6324288 | tf_op jit(solution)/shard_map/add | solution.py:45
  111.5 5.8 %collective-permute-start.21 = (f32[2,1,512]{2,1,0:T(1,128)S(1)}, f32[2,1,512]{2,1,0:T(1,128)S(1)}, u32[]{:S(2)}, u32[]{:S(2)}) collective-permute-start(f32[2,1,512]{2,1,0:T(1,128)S(1)} %get-tuple-element.81), channel_id=1, source_target_pairs={{8,0},{16,8},{24,16},{32,24},{40,32},{48,40},{56,48},{64,56},{72,6... | collective-permute-start | bytes 12296 | tf_op jit(solution)/shard_map/ppermute | solution.py:19
  121.1 3.3 collective-permute-start.23
  127.2 5.0 %fusion.15 = f32[2,512,512]{2,1,0:T(8,128)S(1)} fusion(f32[2,512,512]{2,1,0:T(8,128)S(1)} %copy-done.5, f32[2,514,1]{2,1,0:T(8,128)S(1)} %copy.235, f32[2,1,512]{2,1,0:T(1,128)S(1)} %collective-permute-done.21, f32[2,1,512]{2,1,0:T(1,128)S(1)} %collective-permute-done.20, f32[2,514,1]{2,1,0:T(8,128)S(1)} %copy.234, f32[2,512,514]{2,1,0:T(8,128)S(1)} %slice.612, ...), kind=kLoop, calls=%fused_computation.49 | loop fusion | flops 8912896 | bytes 6324288 | tf_op jit(solution)/shard_map/add | solution.py:45
  132.3 5.8 %collective-permute-start.25 = (f32[2,1,512]{2,1,0:T(1,128)S(1)}, f32[2,1,512]{2,1,0:T(1,128)S(1)}, u32[]{:S(2)}, u32[]{:S(2)}) collective-permute-start(f32[2,1,512]{2,1,0:T(1,128)S(1)} %get-tuple-element.79), channel_id=1, source_target_pairs={{8,0},{16,8},{24,16},{32,24},{40,32},{48,40},{56,48},{64,56},{72,6... | collective-permute-start | bytes 12296 | tf_op jit(solution)/shard_map/ppermute | solution.py:19
  141.9 2.8 collective-permute-start.27
  149.0 4.9 %fusion.9 = f32[2,512,512]{2,1,0:T(8,128)S(1)} fusion(f32[2,512,512]{2,1,0:T(8,128)S(1)} %copy-done.8, f32[2,514,1]{2,1,0:T(8,128)S(1)} %copy.241, f32[2,1,512]{2,1,0:T(1,128)S(1)} %collective-permute-done.25, f32[2,1,512]{2,1,0:T(1,128)S(1)} %collective-permute-done.24, f32[2,514,1]{2,1,0:T(8,128)S(1)} %copy.240, f32[2,512,514]{2,1,0:T(8,128)S(1)} %slice.615, ...), kind=kLoop, calls=%fused_computation.33 | loop fusion | flops 8912896 | bytes 6324288 | tf_op jit(solution)/shard_map/add | solution.py:45
  154.1 5.8 %collective-permute-start.29 = (f32[2,1,512]{2,1,0:T(1,128)S(1)}, f32[2,1,512]{2,1,0:T(1,128)S(1)}, u32[]{:S(2)}, u32[]{:S(2)}) collective-permute-start(f32[2,1,512]{2,1,0:T(1,128)S(1)} %get-tuple-element.77), channel_id=1, source_target_pairs={{8,0},{16,8},{24,16},{32,24},{40,32},{48,40},{56,48},{64,56},{72,6... | collective-permute-start | bytes 12296 | tf_op jit(solution)/shard_map/ppermute | solution.py:19
  163.7 3.0 collective-permute-start.31
  169.6 5.9 %fusion.3 = f32[2,512,512]{2,1,0:T(8,128)} fusion(f32[2,512,512]{2,1,0:T(8,128)S(1)} %fusion.9, f32[2,514,1]{2,1,0:T(8,128)S(1)} %copy.247, f32[2,1,512]{2,1,0:T(1,128)S(1)} %collective-permute-done.29, f32[2,1,512]{2,1,0:T(1,128)S(1)} %collective-permute-done.28, f32[2,514,1]{2,1,0:T(8,128)S(1)} %copy.246, f32[2,512,514]{2,1,0:T(8,128)S(1)} %slice.618, ...), kind=kLoop, calls=%fused_computation.17 | loop fusion | flops 8912896 | bytes 6324288 | tf_op jit(solution)/shard_map/add | solution.py:45
  175.5 71.4 %reshape.326 = f32[2,128,4,128,4]{4,3,2,1,0:T(8,128)} reshape(f32[2,512,512]{2,1,0:T(8,128)} %fusion.3) | data formatting | bytes 4194304 | tf_op jit(solution)/shard_map/reshape | solution.py:104
  246.9 20.8 %reduce_sum.19 = f32[2,128,128]{2,1,0:T(8,128)S(1)} reduce(f32[2,128,4,128,4]{4,3,2,1,0:T(8,128)} %reshape.326, f32[]{:T(128)} %constant.89.clone.1), dimensions={2,4}, to_apply=%region_1.2 | reduce | flops 491520 | bytes 2228228 | tf_op jit(solution)/shard_map/reduce_sum | solution.py:104
  267.8 5.7 %collective-permute-start.33 = (f32[2,1,128]{2,1,0:T(1,128)S(1)}, f32[2,1,128]{2,1,0:T(1,128)S(1)}, u32[]{:S(2)}, u32[]{:S(2)}) collective-permute-start(f32[2,1,128]{2,1,0:T(1,128)S(1)} %get-tuple-element.113), channel_id=1, source_target_pairs={{8,0},{16,8},{24,16},{32,24},{40,32},{48,40},{56,48},{64,56},{72,6... | collective-permute-start | bytes 3080 | tf_op jit(solution)/shard_map/ppermute | solution.py:19
  274.4 4.0 %collective-permute-start.34 = (f32[2,130,1]{2,1,0:T(8,128)S(1)}, f32[2,130,1]{2,1,0:T(8,128)S(1)}, u32[]{:S(2)}, u32[]{:S(2)}) collective-permute-start(f32[2,130,1]{2,1,0:T(8,128)S(1)} %get-tuple-element.110), channel_id=1, source_target_pairs={{0,1},{1,2},{2,3},{3,4},{4,5},{5,6},{6,7},{7,0},{8,9},{9,10},{10,1... | collective-permute-start | bytes 3128 | tf_op jit(solution)/shard_map/ppermute | solution.py:17
  279.6 2.4 collective-permute-done.34
  286.9 18.4 %all_to_all.5 = f32[16,5,1024]{2,1,0:T(8,128)S(1)} all-to-all(f32[16,5,1024]{2,1,0:T(8,128)S(1)} %copy.251), channel_id=1, replica_groups=mesh['tile'=16,'col'=8] {'tile'}, dimensions={0} | all-to-all | bytes 655360 | tf_op jit(solution)/shard_map/all_to_all | solution.py:124
  308.6 64.7 %psum.7 = f32[16,16]{1,0:T(8,128)S(1)} all-reduce(f32[16,16]{1,0:T(8,128)S(1)} %convolution_bitcast_fusion), channel_id=1, replica_groups=mesh['tile'=16,'col'=8] {'tile','col'}, use_global_device_ids=true, to_apply=%region_2.3 | all-reduce | flops 256 | bytes 2048 | tf_op jit(solution)/shard_map/psum | solution.py:135
  (226 shorter events, 70.2 us)
Async XLA Ops:
  8.2 10.1 %collective-permute-start.2 = (f32[2,514,1]{1,0,2:T(2,128)S(1)}, f32[2,514,1]{1,0,2:T(2,128)S(1)}, u32[]{:S(2)}, u32[]{:S(2)}) collective-permute-start(f32[2,514,1]{1,0,2:T(2,128)S(1)} %copy.202), channel_id=1, source_target_pairs={{0,1},{1,2},{2,3},{3,4},{4,5},{5,6},{6,7},{7,0},{8,9},{9,10},{10,1... | collective-permute-start | bytes 12344 | tf_op jit(solution)/shard_map/ppermute | solution.py:17
  12.0 6.6 %collective-permute-start.3 = (f32[2,514,1]{1,0,2:T(2,128)S(1)}, f32[2,514,1]{1,0,2:T(2,128)S(1)}, u32[]{:S(2)}, u32[]{:S(2)}) collective-permute-start(f32[2,514,1]{1,0,2:T(2,128)S(1)} %copy.203), channel_id=1, source_target_pairs={{1,0},{2,1},{3,2},{4,3},{5,4},{6,5},{7,6},{0,7},{9,8},{10,9},{11,1... | collective-permute-start | bytes 12344 | tf_op jit(solution)/shard_map/ppermute | solution.py:19
  33.3 6.1 %collective-permute-start.6 = (f32[2,514,1]{1,0,2:T(2,128)S(1)}, f32[2,514,1]{1,0,2:T(2,128)S(1)}, u32[]{:S(2)}, u32[]{:S(2)}) collective-permute-start(f32[2,514,1]{1,0,2:T(2,128)S(1)} %copy.208), channel_id=1, source_target_pairs={{0,1},{1,2},{2,3},{3,4},{4,5},{5,6},{6,7},{7,0},{8,9},{9,10},{10,1... | collective-permute-start | bytes 12344 | tf_op jit(solution)/shard_map/ppermute | solution.py:17
  34.3 5.4 %collective-permute-start.7 = (f32[2,514,1]{1,0,2:T(2,128)S(1)}, f32[2,514,1]{1,0,2:T(2,128)S(1)}, u32[]{:S(2)}, u32[]{:S(2)}) collective-permute-start(f32[2,514,1]{1,0,2:T(2,128)S(1)} %copy.209), channel_id=1, source_target_pairs={{1,0},{2,1},{3,2},{4,3},{5,4},{6,5},{7,6},{0,7},{9,8},{10,9},{11,1... | collective-permute-start | bytes 12344 | tf_op jit(solution)/shard_map/ppermute | solution.py:19
  52.1 4.9 %collective-permute-start.8 = (f32[2,1,512]{2,1,0:T(1,128)S(1)}, f32[2,1,512]{2,1,0:T(1,128)S(1)}, u32[]{:S(2)}, u32[]{:S(2)}) collective-permute-start(f32[2,1,512]{2,1,0:T(1,128)S(1)} %get-tuple-element.86), channel_id=1, source_target_pairs={{0,8},{8,16},{16,24},{24,32},{32,40},{40,48},{48,56},{56,64},{64,7... | collective-permute-start | bytes 12296 | tf_op jit(solution)/shard_map/ppermute | solution.py:17
  53.3 3.8 %collective-permute-start.9 = (f32[2,1,512]{2,1,0:T(1,128)S(1)}, f32[2,1,512]{2,1,0:T(1,128)S(1)}, u32[]{:S(2)}, u32[]{:S(2)}) collective-permute-start(f32[2,1,512]{2,1,0:T(1,128)S(1)} %get-tuple-element.87), channel_id=1, source_target_pairs={{8,0},{16,8},{24,16},{32,24},{40,32},{48,40},{56,48},{64,56},{72,6... | collective-permute-start | bytes 12296 | tf_op jit(solution)/shard_map/ppermute | solution.py:19
  57.6 6.6 %collective-permute-start.10 = (f32[2,514,1]{1,0,2:T(2,128)S(1)}, f32[2,514,1]{1,0,2:T(2,128)S(1)}, u32[]{:S(2)}, u32[]{:S(2)}) collective-permute-start(f32[2,514,1]{1,0,2:T(2,128)S(1)} %copy.214), channel_id=1, source_target_pairs={{0,1},{1,2},{2,3},{3,4},{4,5},{5,6},{6,7},{7,0},{8,9},{9,10},{10,1... | collective-permute-start | bytes 12344 | tf_op jit(solution)/shard_map/ppermute | solution.py:17
  59.6 4.8 %collective-permute-start.11 = (f32[2,514,1]{1,0,2:T(2,128)S(1)}, f32[2,514,1]{1,0,2:T(2,128)S(1)}, u32[]{:S(2)}, u32[]{:S(2)}) collective-permute-start(f32[2,514,1]{1,0,2:T(2,128)S(1)} %copy.215), channel_id=1, source_target_pairs={{1,0},{2,1},{3,2},{4,3},{5,4},{6,5},{7,6},{0,7},{9,8},{10,9},{11,1... | collective-permute-start | bytes 12344 | tf_op jit(solution)/shard_map/ppermute | solution.py:19
  71.1 5.9 %collective-permute-start.12 = (f32[2,1,512]{2,1,0:T(1,128)S(1)}, f32[2,1,512]{2,1,0:T(1,128)S(1)}, u32[]{:S(2)}, u32[]{:S(2)}) collective-permute-start(f32[2,1,512]{2,1,0:T(1,128)S(1)} %get-tuple-element.84), channel_id=1, source_target_pairs={{0,8},{8,16},{16,24},{24,32},{32,40},{40,48},{48,56},{56,64},{64,7... | collective-permute-start | bytes 12296 | tf_op jit(solution)/shard_map/ppermute | solution.py:17
  71.8 5.4 %collective-permute-start.13 = (f32[2,1,512]{2,1,0:T(1,128)S(1)}, f32[2,1,512]{2,1,0:T(1,128)S(1)}, u32[]{:S(2)}, u32[]{:S(2)}) collective-permute-start(f32[2,1,512]{2,1,0:T(1,128)S(1)} %get-tuple-element.85), channel_id=1, source_target_pairs={{8,0},{16,8},{24,16},{32,24},{40,32},{48,40},{56,48},{64,56},{72,6... | collective-permute-start | bytes 12296 | tf_op jit(solution)/shard_map/ppermute | solution.py:19
  77.7 6.4 %collective-permute-start.14 = (f32[2,514,1]{1,0,2:T(2,128)S(1)}, f32[2,514,1]{1,0,2:T(2,128)S(1)}, u32[]{:S(2)}, u32[]{:S(2)}) collective-permute-start(f32[2,514,1]{1,0,2:T(2,128)S(1)} %copy.220), channel_id=1, source_target_pairs={{0,1},{1,2},{2,3},{3,4},{4,5},{5,6},{6,7},{7,0},{8,9},{9,10},{10,1... | collective-permute-start | bytes 12344 | tf_op jit(solution)/shard_map/ppermute | solution.py:17
  79.9 4.4 %collective-permute-start.15 = (f32[2,514,1]{1,0,2:T(2,128)S(1)}, f32[2,514,1]{1,0,2:T(2,128)S(1)}, u32[]{:S(2)}, u32[]{:S(2)}) collective-permute-start(f32[2,514,1]{1,0,2:T(2,128)S(1)} %copy.221), channel_id=1, source_target_pairs={{1,0},{2,1},{3,2},{4,3},{5,4},{6,5},{7,6},{0,7},{9,8},{10,9},{11,1... | collective-permute-start | bytes 12344 | tf_op jit(solution)/shard_map/ppermute | solution.py:19
  90.9 6.3 %collective-permute-start.16 = (f32[2,1,512]{2,1,0:T(1,128)S(1)}, f32[2,1,512]{2,1,0:T(1,128)S(1)}, u32[]{:S(2)}, u32[]{:S(2)}) collective-permute-start(f32[2,1,512]{2,1,0:T(1,128)S(1)} %get-tuple-element.82), channel_id=1, source_target_pairs={{0,8},{8,16},{16,24},{24,32},{32,40},{40,48},{48,56},{56,64},{64,7... | collective-permute-start | bytes 12296 | tf_op jit(solution)/shard_map/ppermute | solution.py:17
  91.0 6.4 %collective-permute-start.17 = (f32[2,1,512]{2,1,0:T(1,128)S(1)}, f32[2,1,512]{2,1,0:T(1,128)S(1)}, u32[]{:S(2)}, u32[]{:S(2)}) collective-permute-start(f32[2,1,512]{2,1,0:T(1,128)S(1)} %get-tuple-element.83), channel_id=1, source_target_pairs={{8,0},{16,8},{24,16},{32,24},{40,32},{48,40},{56,48},{64,56},{72,6... | collective-permute-start | bytes 12296 | tf_op jit(solution)/shard_map/ppermute | solution.py:19
  97.9 6.3 %collective-permute-start.18 = (f32[2,514,1]{1,0,2:T(2,128)S(1)}, f32[2,514,1]{1,0,2:T(2,128)S(1)}, u32[]{:S(2)}, u32[]{:S(2)}) collective-permute-start(f32[2,514,1]{1,0,2:T(2,128)S(1)} %copy.226), channel_id=1, source_target_pairs={{0,1},{1,2},{2,3},{3,4},{4,5},{5,6},{6,7},{7,0},{8,9},{9,10},{10,1... | collective-permute-start | bytes 12344 | tf_op jit(solution)/shard_map/ppermute | solution.py:17
  100.8 4.0 %collective-permute-start.19 = (f32[2,514,1]{1,0,2:T(2,128)S(1)}, f32[2,514,1]{1,0,2:T(2,128)S(1)}, u32[]{:S(2)}, u32[]{:S(2)}) collective-permute-start(f32[2,514,1]{1,0,2:T(2,128)S(1)} %copy.227), channel_id=1, source_target_pairs={{1,0},{2,1},{3,2},{4,3},{5,4},{6,5},{7,6},{0,7},{9,8},{10,9},{11,1... | collective-permute-start | bytes 12344 | tf_op jit(solution)/shard_map/ppermute | solution.py:19
  111.4 6.4 %collective-permute-start.20 = (f32[2,1,512]{2,1,0:T(1,128)S(1)}, f32[2,1,512]{2,1,0:T(1,128)S(1)}, u32[]{:S(2)}, u32[]{:S(2)}) collective-permute-start(f32[2,1,512]{2,1,0:T(1,128)S(1)} %get-tuple-element.80), channel_id=1, source_target_pairs={{0,8},{8,16},{16,24},{24,32},{32,40},{40,48},{48,56},{56,64},{64,7... | collective-permute-start | bytes 12296 | tf_op jit(solution)/shard_map/ppermute | solution.py:17
  111.5 6.6 %collective-permute-start.21 = (f32[2,1,512]{2,1,0:T(1,128)S(1)}, f32[2,1,512]{2,1,0:T(1,128)S(1)}, u32[]{:S(2)}, u32[]{:S(2)}) collective-permute-start(f32[2,1,512]{2,1,0:T(1,128)S(1)} %get-tuple-element.81), channel_id=1, source_target_pairs={{8,0},{16,8},{24,16},{32,24},{40,32},{48,40},{56,48},{64,56},{72,6... | collective-permute-start | bytes 12296 | tf_op jit(solution)/shard_map/ppermute | solution.py:19
  118.6 6.1 %collective-permute-start.22 = (f32[2,514,1]{1,0,2:T(2,128)S(1)}, f32[2,514,1]{1,0,2:T(2,128)S(1)}, u32[]{:S(2)}, u32[]{:S(2)}) collective-permute-start(f32[2,514,1]{1,0,2:T(2,128)S(1)} %copy.232), channel_id=1, source_target_pairs={{0,1},{1,2},{2,3},{3,4},{4,5},{5,6},{6,7},{7,0},{8,9},{9,10},{10,1... | collective-permute-start | bytes 12344 | tf_op jit(solution)/shard_map/ppermute | solution.py:17
  121.1 4.5 %collective-permute-start.23 = (f32[2,514,1]{1,0,2:T(2,128)S(1)}, f32[2,514,1]{1,0,2:T(2,128)S(1)}, u32[]{:S(2)}, u32[]{:S(2)}) collective-permute-start(f32[2,514,1]{1,0,2:T(2,128)S(1)} %copy.233), channel_id=1, source_target_pairs={{1,0},{2,1},{3,2},{4,3},{5,4},{6,5},{7,6},{0,7},{9,8},{10,9},{11,1... | collective-permute-start | bytes 12344 | tf_op jit(solution)/shard_map/ppermute | solution.py:19
  132.2 6.4 %collective-permute-start.24 = (f32[2,1,512]{2,1,0:T(1,128)S(1)}, f32[2,1,512]{2,1,0:T(1,128)S(1)}, u32[]{:S(2)}, u32[]{:S(2)}) collective-permute-start(f32[2,1,512]{2,1,0:T(1,128)S(1)} %get-tuple-element.78), channel_id=1, source_target_pairs={{0,8},{8,16},{16,24},{24,32},{32,40},{40,48},{48,56},{56,64},{64,7... | collective-permute-start | bytes 12296 | tf_op jit(solution)/shard_map/ppermute | solution.py:17
  132.3 6.6 %collective-permute-start.25 = (f32[2,1,512]{2,1,0:T(1,128)S(1)}, f32[2,1,512]{2,1,0:T(1,128)S(1)}, u32[]{:S(2)}, u32[]{:S(2)}) collective-permute-start(f32[2,1,512]{2,1,0:T(1,128)S(1)} %get-tuple-element.79), channel_id=1, source_target_pairs={{8,0},{16,8},{24,16},{32,24},{40,32},{48,40},{56,48},{64,56},{72,6... | collective-permute-start | bytes 12296 | tf_op jit(solution)/shard_map/ppermute | solution.py:19
  139.3 6.1 %collective-permute-start.26 = (f32[2,514,1]{1,0,2:T(2,128)S(1)}, f32[2,514,1]{1,0,2:T(2,128)S(1)}, u32[]{:S(2)}, u32[]{:S(2)}) collective-permute-start(f32[2,514,1]{1,0,2:T(2,128)S(1)} %copy.238), channel_id=1, source_target_pairs={{0,1},{1,2},{2,3},{3,4},{4,5},{5,6},{6,7},{7,0},{8,9},{9,10},{10,1... | collective-permute-start | bytes 12344 | tf_op jit(solution)/shard_map/ppermute | solution.py:17
  141.9 4.0 %collective-permute-start.27 = (f32[2,514,1]{1,0,2:T(2,128)S(1)}, f32[2,514,1]{1,0,2:T(2,128)S(1)}, u32[]{:S(2)}, u32[]{:S(2)}) collective-permute-start(f32[2,514,1]{1,0,2:T(2,128)S(1)} %copy.239), channel_id=1, source_target_pairs={{1,0},{2,1},{3,2},{4,3},{5,4},{6,5},{7,6},{0,7},{9,8},{10,9},{11,1... | collective-permute-start | bytes 12344 | tf_op jit(solution)/shard_map/ppermute | solution.py:19
  154.0 6.4 %collective-permute-start.28 = (f32[2,1,512]{2,1,0:T(1,128)S(1)}, f32[2,1,512]{2,1,0:T(1,128)S(1)}, u32[]{:S(2)}, u32[]{:S(2)}) collective-permute-start(f32[2,1,512]{2,1,0:T(1,128)S(1)} %get-tuple-element.76), channel_id=1, source_target_pairs={{0,8},{8,16},{16,24},{24,32},{32,40},{40,48},{48,56},{56,64},{64,7... | collective-permute-start | bytes 12296 | tf_op jit(solution)/shard_map/ppermute | solution.py:17
  154.1 6.6 %collective-permute-start.29 = (f32[2,1,512]{2,1,0:T(1,128)S(1)}, f32[2,1,512]{2,1,0:T(1,128)S(1)}, u32[]{:S(2)}, u32[]{:S(2)}) collective-permute-start(f32[2,1,512]{2,1,0:T(1,128)S(1)} %get-tuple-element.77), channel_id=1, source_target_pairs={{8,0},{16,8},{24,16},{32,24},{40,32},{48,40},{56,48},{64,56},{72,6... | collective-permute-start | bytes 12296 | tf_op jit(solution)/shard_map/ppermute | solution.py:19
  161.1 6.1 %collective-permute-start.30 = (f32[2,514,1]{1,0,2:T(2,128)S(1)}, f32[2,514,1]{1,0,2:T(2,128)S(1)}, u32[]{:S(2)}, u32[]{:S(2)}) collective-permute-start(f32[2,514,1]{1,0,2:T(2,128)S(1)} %copy.244), channel_id=1, source_target_pairs={{0,1},{1,2},{2,3},{3,4},{4,5},{5,6},{6,7},{7,0},{8,9},{9,10},{10,1... | collective-permute-start | bytes 12344 | tf_op jit(solution)/shard_map/ppermute | solution.py:17
  163.7 4.3 %collective-permute-start.31 = (f32[2,514,1]{1,0,2:T(2,128)S(1)}, f32[2,514,1]{1,0,2:T(2,128)S(1)}, u32[]{:S(2)}, u32[]{:S(2)}) collective-permute-start(f32[2,514,1]{1,0,2:T(2,128)S(1)} %copy.245), channel_id=1, source_target_pairs={{1,0},{2,1},{3,2},{4,3},{5,4},{6,5},{7,6},{0,7},{9,8},{10,9},{11,1... | collective-permute-start | bytes 12344 | tf_op jit(solution)/shard_map/ppermute | solution.py:19
  267.7 6.3 %collective-permute-start.32 = (f32[2,1,128]{2,1,0:T(1,128)S(1)}, f32[2,1,128]{2,1,0:T(1,128)S(1)}, u32[]{:S(2)}, u32[]{:S(2)}) collective-permute-start(f32[2,1,128]{2,1,0:T(1,128)S(1)} %get-tuple-element.112), channel_id=1, source_target_pairs={{0,8},{8,16},{16,24},{24,32},{32,40},{40,48},{48,56},{56,64},{64,7... | collective-permute-start | bytes 3080 | tf_op jit(solution)/shard_map/ppermute | solution.py:17
  267.8 6.5 %collective-permute-start.33 = (f32[2,1,128]{2,1,0:T(1,128)S(1)}, f32[2,1,128]{2,1,0:T(1,128)S(1)}, u32[]{:S(2)}, u32[]{:S(2)}) collective-permute-start(f32[2,1,128]{2,1,0:T(1,128)S(1)} %get-tuple-element.113), channel_id=1, source_target_pairs={{8,0},{16,8},{24,16},{32,24},{40,32},{48,40},{56,48},{64,56},{72,6... | collective-permute-start | bytes 3080 | tf_op jit(solution)/shard_map/ppermute | solution.py:19
  274.4 7.6 %collective-permute-start.34 = (f32[2,130,1]{2,1,0:T(8,128)S(1)}, f32[2,130,1]{2,1,0:T(8,128)S(1)}, u32[]{:S(2)}, u32[]{:S(2)}) collective-permute-start(f32[2,130,1]{2,1,0:T(8,128)S(1)} %get-tuple-element.110), channel_id=1, source_target_pairs={{0,1},{1,2},{2,3},{3,4},{4,5},{5,6},{6,7},{7,0},{8,9},{9,10},{10,1... | collective-permute-start | bytes 3128 | tf_op jit(solution)/shard_map/ppermute | solution.py:17
  278.5 5.4 %collective-permute-start.35 = (f32[2,130,1]{2,1,0:T(8,128)S(1)}, f32[2,130,1]{2,1,0:T(8,128)S(1)}, u32[]{:S(2)}, u32[]{:S(2)}) collective-permute-start(f32[2,130,1]{2,1,0:T(8,128)S(1)} %get-tuple-element.111), channel_id=1, source_target_pairs={{1,0},{2,1},{3,2},{4,3},{5,4},{6,5},{7,6},{0,7},{9,8},{10,9},{11,1... | collective-permute-start | bytes 3128 | tf_op jit(solution)/shard_map/ppermute | solution.py:19
  (25 other events, 210.2 us)
where the time goes:
time: 381 us; the launch traced here: 374 us
  starting transfers between devices  91.9 us (24%)
  local copies, waits for them, and re-layouts  89.5 us (23%)
  blocking collectives  83.1 us (22%)
  other arithmetic  81.8 us (21%)
  waiting for transfers between devices  20.8 us (5%)
  between operations  5.18 us (1%)
    reshape x1, local copies, waits for them, and re-layouts, per_device(): field.reshape(2, fine_rows // 4, 4, fine_cols // 4, 4).mean(axis=(2, 4))  71.4 us
    psum x1, blocking collectives, per_device(): gram = lax.psum(part, ('tile', 'col')) / (fine_rows // 4 * (fine_cols // 4))  64.7 us
    ppermute x18, starting transfers between devices, with_halo(): lax.ppermute(head, axis, [((i + 1) % count, i) for i in range(count)])  64.6 us
    add x8, other arithmetic, relax(): return centre + KAPPA * (beside_all - 4.0 * centre)  45.1 us
    ppermute x18, starting transfers between devices, with_halo(): lax.ppermute(tail, axis, [(i, (i + 1) % count) for i in range(count)])  27.3 us
    reduce_sum x1, other arithmetic, per_device(): field.reshape(2, fine_rows // 4, 4, fine_cols // 4, 4).mean(axis=(2, 4))  20.8 us
    all_to_all x1, blocking collectives, per_device(): lax.all_to_all(jnp.einsum('vh,hsd->vsd', chosen_terms, starting_tile_set,...  18.4 us
    ppermute x18, waiting for transfers between devices, with_halo(): lax.ppermute(tail, axis, [(i, (i + 1) % count) for i in range(count)])  11.6 us
  transfers between devices with their start and end apart: 36, of which 31 were waited for; matrix products, arithmetic and copies ran while one was open for 1% of the time, Pallas kernels for 0%

commit v1 on v0

--- a/solution.py
+++ b/solution.py
@@ -5,6 +5,11 @@
 
 PASSES = 8
 KAPPA = 0.2
+
+
+def by_each_axis(value, inner_axis, outer_axis):
+    half = lax.psum(value, inner_axis)
+    return lax.psum(half, outer_axis)
 
 
 def with_halo(cells, sides, width):
@@ -132,7 +137,7 @@
         )
     )
     part = jnp.einsum("pnc,pmc->nm", library, library, precision=lax.Precision.HIGHEST)
-    gram = lax.psum(part, ("tile", "col")) / (fine_rows // 4 * (fine_cols // 4))
+    gram = by_each_axis(part, "col", "tile") / (fine_rows // 4 * (fine_cols // 4))
     return (library[None, None], gram)
 
 

time: 381 us -> 368 us (0.966)
  blocking collectives: 83.1 us -> 70.4 us
    psum x1 -> x2, blocking collectives: 64.7 us -> 52 us  [the longest x1 32 us: by_each_axis(): return lax.psum(half, outer_axis)]
where the time goes in v1:
time: 368 us; the launch traced here: 361 us
  starting transfers between devices  91.8 us (25%)
  local copies, waits for them, and re-layouts  89.5 us (24%)
  other arithmetic  81.8 us (22%)
  blocking collectives  70.4 us (19%)
  waiting for transfers between devices  20.8 us (6%)
  between operations  5.21 us (1%)
    reshape x1, local copies, waits for them, and re-layouts, per_device(): field.reshape(2, fine_rows // 4, 4, fine_cols // 4, 4).mean(axis=(2, 4))  71.4 us
    ppermute x18, starting transfers between devices, with_halo(): lax.ppermute(head, axis, [((i + 1) % count, i) for i in range(count)])  64.6 us
    add x8, other arithmetic, relax(): return centre + KAPPA * (beside_all - 4.0 * centre)  45.1 us
    psum x1, blocking collectives, by_each_axis(): return lax.psum(half, outer_axis)  32 us
    ppermute x18, starting transfers between devices, with_halo(): lax.ppermute(tail, axis, [(i, (i + 1) % count) for i in range(count)])  27.3 us
    reduce_sum x1, other arithmetic, per_device(): field.reshape(2, fine_rows // 4, 4, fine_cols // 4, 4).mean(axis=(2, 4))  20.8 us
    psum x1, blocking collectives, by_each_axis(): half = lax.psum(value, inner_axis)  20 us
    all_to_all x1, blocking collectives, per_device(): lax.all_to_all(jnp.einsum('vh,hsd->vsd', chosen_terms, starting_tile_set,...  18.4 us
  transfers between devices with their start and end apart: 36, of which 31 were waited for; matrix products, arithmetic and copies ran while one was open for 1% of the time, Pallas kernels for 0%

profile of v1, /device:TPU:1, one launch (start us, length us, event | category | flops | bytes accessed | tf_op | source)
XLA Modules:
  0.0 361.3 jit_solution(17026217738489612826)
XLA Ops:
  1.6 3.1 collective-permute-start
  8.2 3.5 collective-permute-start.2
  12.0 2.5 collective-permute-start.3
  21.4 6.4 %fusion.45 = f32[2,512,512]{2,1,0:T(8,128)S(1)} fusion(f32[2,514,1]{2,1,0:T(8,128)} %copy-done.15, f32[2,1,512]{2,1,0:T(1,128)S(1)} %collective-permute-done.1, f32[2,1,512]{2,1,0:T(1,128)S(1)} %collective-permute-done, f32[1,512,512]{2,1,0:T(8,128)S(1)} %bitcast.34, f32[1,512,512]{2,1,0:T(8,128)S(1)} %bitcast.28, f32[2,514,1]{2,1,0:T(8,128)} %copy-done.13, ...), kind=kLoop, calls=%fused_computation.129 | loop fusion | flops 10485760 | bytes 6324288 | tf_op jit(solution)/shard_map/add | solution.py:50
  34.3 4.6 %collective-permute-start.7 = (f32[2,514,1]{1,0,2:T(2,128)S(1)}, f32[2,514,1]{1,0,2:T(2,128)S(1)}, u32[]{:S(2)}, u32[]{:S(2)}) collective-permute-start(f32[2,514,1]{1,0,2:T(2,128)S(1)} %copy.209), channel_id=1, source_target_pairs={{1,0},{2,1},{3,2},{4,3},{5,4},{6,5},{7,6},{0,7},{9,8},{10,9},{11,1... | collective-permute-start | bytes 12344 | tf_op jit(solution)/shard_map/ppermute | solution.py:24
  44.0 8.1 %fusion.39 = f32[2,512,512]{2,1,0:T(8,128)S(1)} fusion(f32[2,512,512]{2,1,0:T(8,128)} %copy-done.9, f32[2,514,1]{2,1,0:T(8,128)S(1)} %copy-done.16, f32[2,1,512]{2,1,0:T(1,128)S(1)} %collective-permute-done.5, f32[2,1,512]{2,1,0:T(1,128)S(1)} %collective-permute-done.4, f32[2,514,1]{2,1,0:T(8,128)} %copy-done.14, f32[2,512,514]{2,1,0:T(8,128)S(1)} %slice.600, ...), kind=kLoop, calls=%fused_computation.113 | loop fusion | flops 8912896 | bytes 6324288 | tf_op jit(solution)/shard_map/add | solution.py:50
  53.3 3.0 collective-permute-start.9
  59.6 3.8 %collective-permute-start.11 = (f32[2,514,1]{1,0,2:T(2,128)S(1)}, f32[2,514,1]{1,0,2:T(2,128)S(1)}, u32[]{:S(2)}, u32[]{:S(2)}) collective-permute-start(f32[2,514,1]{1,0,2:T(2,128)S(1)} %copy.215), channel_id=1, source_target_pairs={{1,0},{2,1},{3,2},{4,3},{5,4},{6,5},{7,6},{0,7},{9,8},{10,9},{11,1... | collective-permute-start | bytes 12344 | tf_op jit(solution)/shard_map/ppermute | solution.py:24
  66.1 5.0 %fusion.33 = f32[2,512,512]{2,1,0:T(8,128)S(1)} fusion(f32[2,512,512]{2,1,0:T(8,128)S(1)} %fusion.39, f32[2,514,1]{2,1,0:T(8,128)S(1)} %copy.217, f32[2,1,512]{2,1,0:T(1,128)S(1)} %collective-permute-done.9, f32[2,1,512]{2,1,0:T(1,128)S(1)} %collective-permute-done.8, f32[2,514,1]{2,1,0:T(8,128)S(1)} %copy.216, f32[2,512,514]{2,1,0:T(8,128)S(1)} %slice.603, ...), kind=kLoop, calls=%fused_computation.97 | loop fusion | flops 8912896 | bytes 6324288 | tf_op jit(solution)/shard_map/add | solution.py:50
  71.8 4.6 %collective-permute-start.13 = (f32[2,1,512]{2,1,0:T(1,128)S(1)}, f32[2,1,512]{2,1,0:T(1,128)S(1)}, u32[]{:S(2)}, u32[]{:S(2)}) collective-permute-start(f32[2,1,512]{2,1,0:T(1,128)S(1)} %get-tuple-element.85), channel_id=1, source_target_pairs={{8,0},{16,8},{24,16},{32,24},{40,32},{48,40},{56,48},{64,56},{72,6... | collective-permute-start | bytes 12296 | tf_op jit(solution)/shard_map/ppermute | solution.py:24
  79.9 3.6 %collective-permute-start.15 = (f32[2,514,1]{1,0,2:T(2,128)S(1)}, f32[2,514,1]{1,0,2:T(2,128)S(1)}, u32[]{:S(2)}, u32[]{:S(2)}) collective-permute-start(f32[2,514,1]{1,0,2:T(2,128)S(1)} %copy.221), channel_id=1, source_target_pairs={{1,0},{2,1},{3,2},{4,3},{5,4},{6,5},{7,6},{0,7},{9,8},{10,9},{11,1... | collective-permute-start | bytes 12344 | tf_op jit(solution)/shard_map/ppermute | solution.py:24
  86.0 5.0 %fusion.27 = f32[2,512,512]{2,1,0:T(8,128)S(1)} fusion(f32[2,512,512]{2,1,0:T(8,128)S(1)} %copy-done.1, f32[2,514,1]{2,1,0:T(8,128)S(1)} %copy.223, f32[2,1,512]{2,1,0:T(1,128)S(1)} %collective-permute-done.13, f32[2,1,512]{2,1,0:T(1,128)S(1)} %collective-permute-done.12, f32[2,514,1]{2,1,0:T(8,128)S(1)} %copy.222, f32[2,512,514]{2,1,0:T(8,128)S(1)} %slice.606, ...), kind=kLoop, calls=%fused_computation.81 | loop fusion | flops 8912896 | bytes 6324288 | tf_op jit(solution)/shard_map/add | solution.py:50
  91.0 5.6 %collective-permute-start.17 = (f32[2,1,512]{2,1,0:T(1,128)S(1)}, f32[2,1,512]{2,1,0:T(1,128)S(1)}, u32[]{:S(2)}, u32[]{:S(2)}) collective-permute-start(f32[2,1,512]{2,1,0:T(1,128)S(1)} %get-tuple-element.83), channel_id=1, source_target_pairs={{8,0},{16,8},{24,16},{32,24},{40,32},{48,40},{56,48},{64,56},{72,6... | collective-permute-start | bytes 12296 | tf_op jit(solution)/shard_map/ppermute | solution.py:24
  97.9 2.7 collective-permute-start.18
  100.8 2.7 collective-permute-start.19
  106.4 5.0 %fusion.21 = f32[2,512,512]{2,1,0:T(8,128)S(1)} fusion(f32[2,512,512]{2,1,0:T(8,128)S(1)} %copy-done.3, f32[2,514,1]{2,1,0:T(8,128)S(1)} %copy.229, f32[2,1,512]{2,1,0:T(1,128)S(1)} %collective-permute-done.17, f32[2,1,512]{2,1,0:T(1,128)S(1)} %collective-permute-done.16, f32[2,514,1]{2,1,0:T(8,128)S(1)} %copy.228, f32[2,512,514]{2,1,0:T(8,128)S(1)} %slice.609, ...), kind=kLoop, calls=%fused_computation.65 | loop fusion | flops 8912896 | bytes 6324288 | tf_op jit(solution)/shard_map/add | solution.py:50
  111.5 5.8 %collective-permute-start.21 = (f32[2,1,512]{2,1,0:T(1,128)S(1)}, f32[2,1,512]{2,1,0:T(1,128)S(1)}, u32[]{:S(2)}, u32[]{:S(2)}) collective-permute-start(f32[2,1,512]{2,1,0:T(1,128)S(1)} %get-tuple-element.81), channel_id=1, source_target_pairs={{8,0},{16,8},{24,16},{32,24},{40,32},{48,40},{56,48},{64,56},{72,6... | collective-permute-start | bytes 12296 | tf_op jit(solution)/shard_map/ppermute | solution.py:24
  121.1 3.3 collective-permute-start.23
  127.1 5.0 %fusion.15 = f32[2,512,512]{2,1,0:T(8,128)S(1)} fusion(f32[2,512,512]{2,1,0:T(8,128)S(1)} %copy-done.5, f32[2,514,1]{2,1,0:T(8,128)S(1)} %copy.235, f32[2,1,512]{2,1,0:T(1,128)S(1)} %collective-permute-done.21, f32[2,1,512]{2,1,0:T(1,128)S(1)} %collective-permute-done.20, f32[2,514,1]{2,1,0:T(8,128)S(1)} %copy.234, f32[2,512,514]{2,1,0:T(8,128)S(1)} %slice.612, ...), kind=kLoop, calls=%fused_computation.49 | loop fusion | flops 8912896 | bytes 6324288 | tf_op jit(solution)/shard_map/add | solution.py:50
  132.2 5.8 %collective-permute-start.25 = (f32[2,1,512]{2,1,0:T(1,128)S(1)}, f32[2,1,512]{2,1,0:T(1,128)S(1)}, u32[]{:S(2)}, u32[]{:S(2)}) collective-permute-start(f32[2,1,512]{2,1,0:T(1,128)S(1)} %get-tuple-element.79), channel_id=1, source_target_pairs={{8,0},{16,8},{24,16},{32,24},{40,32},{48,40},{56,48},{64,56},{72,6... | collective-permute-start | bytes 12296 | tf_op jit(solution)/shard_map/ppermute | solution.py:24
  141.9 2.8 collective-permute-start.27
  149.0 4.9 %fusion.9 = f32[2,512,512]{2,1,0:T(8,128)S(1)} fusion(f32[2,512,512]{2,1,0:T(8,128)S(1)} %copy-done.8, f32[2,514,1]{2,1,0:T(8,128)S(1)} %copy.241, f32[2,1,512]{2,1,0:T(1,128)S(1)} %collective-permute-done.25, f32[2,1,512]{2,1,0:T(1,128)S(1)} %collective-permute-done.24, f32[2,514,1]{2,1,0:T(8,128)S(1)} %copy.240, f32[2,512,514]{2,1,0:T(8,128)S(1)} %slice.615, ...), kind=kLoop, calls=%fused_computation.33 | loop fusion | flops 8912896 | bytes 6324288 | tf_op jit(solution)/shard_map/add | solution.py:50
  154.0 5.8 %collective-permute-start.29 = (f32[2,1,512]{2,1,0:T(1,128)S(1)}, f32[2,1,512]{2,1,0:T(1,128)S(1)}, u32[]{:S(2)}, u32[]{:S(2)}) collective-permute-start(f32[2,1,512]{2,1,0:T(1,128)S(1)} %get-tuple-element.77), channel_id=1, source_target_pairs={{8,0},{16,8},{24,16},{32,24},{40,32},{48,40},{56,48},{64,56},{72,6... | collective-permute-start | bytes 12296 | tf_op jit(solution)/shard_map/ppermute | solution.py:24
  163.6 3.0 collective-permute-start.31
  169.5 5.9 %fusion.3 = f32[2,512,512]{2,1,0:T(8,128)} fusion(f32[2,512,512]{2,1,0:T(8,128)S(1)} %fusion.9, f32[2,514,1]{2,1,0:T(8,128)S(1)} %copy.247, f32[2,1,512]{2,1,0:T(1,128)S(1)} %collective-permute-done.29, f32[2,1,512]{2,1,0:T(1,128)S(1)} %collective-permute-done.28, f32[2,514,1]{2,1,0:T(8,128)S(1)} %copy.246, f32[2,512,514]{2,1,0:T(8,128)S(1)} %slice.618, ...), kind=kLoop, calls=%fused_computation.17 | loop fusion | flops 8912896 | bytes 6324288 | tf_op jit(solution)/shard_map/add | solution.py:50
  175.4 71.4 %reshape.326 = f32[2,128,4,128,4]{4,3,2,1,0:T(8,128)} reshape(f32[2,512,512]{2,1,0:T(8,128)} %fusion.3) | data formatting | bytes 4194304 | tf_op jit(solution)/shard_map/reshape | solution.py:109
  246.9 20.8 %reduce_sum.19 = f32[2,128,128]{2,1,0:T(8,128)S(1)} reduce(f32[2,128,4,128,4]{4,3,2,1,0:T(8,128)} %reshape.326, f32[]{:T(128)} %constant.89.clone.1), dimensions={2,4}, to_apply=%region_1.2 | reduce | flops 491520 | bytes 2228228 | tf_op jit(solution)/shard_map/reduce_sum | solution.py:109
  267.7 5.7 %collective-permute-start.33 = (f32[2,1,128]{2,1,0:T(1,128)S(1)}, f32[2,1,128]{2,1,0:T(1,128)S(1)}, u32[]{:S(2)}, u32[]{:S(2)}) collective-permute-start(f32[2,1,128]{2,1,0:T(1,128)S(1)} %get-tuple-element.113), channel_id=1, source_target_pairs={{8,0},{16,8},{24,16},{32,24},{40,32},{48,40},{56,48},{64,56},{72,6... | collective-permute-start | bytes 3080 | tf_op jit(solution)/shard_map/ppermute | solution.py:24
  274.4 4.0 %collective-permute-start.34 = (f32[2,130,1]{2,1,0:T(8,128)S(1)}, f32[2,130,1]{2,1,0:T(8,128)S(1)}, u32[]{:S(2)}, u32[]{:S(2)}) collective-permute-start(f32[2,130,1]{2,1,0:T(8,128)S(1)} %get-tuple-element.110), channel_id=1, source_target_pairs={{0,1},{1,2},{2,3},{3,4},{4,5},{5,6},{6,7},{7,0},{8,9},{9,10},{10,1... | collective-permute-start | bytes 3128 | tf_op jit(solution)/shard_map/ppermute | solution.py:22
  286.8 18.4 %all_to_all.5 = f32[16,5,1024]{2,1,0:T(8,128)S(1)} all-to-all(f32[16,5,1024]{2,1,0:T(8,128)S(1)} %copy.251), channel_id=1, replica_groups=mesh['tile'=16,'col'=8] {'tile'}, dimensions={0} | all-to-all | bytes 655360 | tf_op jit(solution)/shard_map/all_to_all | solution.py:129
  308.5 20.0 %psum.14 = f32[16,16]{1,0:T(8,128)S(1)} all-reduce(f32[16,16]{1,0:T(8,128)S(1)} %convolution_bitcast_fusion), channel_id=1, replica_groups=mesh['tile'=16,'col'=8] {'col'}, use_global_device_ids=true, to_apply=%region_2.3 | all-reduce | flops 256 | bytes 2048 | tf_op jit(solution)/shard_map/psum | solution.py:11
  328.5 32.0 %psum.15 = f32[16,16]{1,0:T(8,128)S(1)} all-reduce(f32[16,16]{1,0:T(8,128)S(1)} %psum.14), channel_id=1, replica_groups=mesh['tile'=16,'col'=8] {'tile'}, use_global_device_ids=true, to_apply=%region_3.4 | all-reduce | flops 256 | bytes 2048 | tf_op jit(solution)/shard_map/psum | solution.py:12
  (227 shorter events, 72.6 us)
Async XLA Ops:
  8.2 10.1 %collective-permute-start.2 = (f32[2,514,1]{1,0,2:T(2,128)S(1)}, f32[2,514,1]{1,0,2:T(2,128)S(1)}, u32[]{:S(2)}, u32[]{:S(2)}) collective-permute-start(f32[2,514,1]{1,0,2:T(2,128)S(1)} %copy.202), channel_id=1, source_target_pairs={{0,1},{1,2},{2,3},{3,4},{4,5},{5,6},{6,7},{7,0},{8,9},{9,10},{10,1... | collective-permute-start | bytes 12344 | tf_op jit(solution)/shard_map/ppermute | solution.py:22
  12.0 6.6 %collective-permute-start.3 = (f32[2,514,1]{1,0,2:T(2,128)S(1)}, f32[2,514,1]{1,0,2:T(2,128)S(1)}, u32[]{:S(2)}, u32[]{:S(2)}) collective-permute-start(f32[2,514,1]{1,0,2:T(2,128)S(1)} %copy.203), channel_id=1, source_target_pairs={{1,0},{2,1},{3,2},{4,3},{5,4},{6,5},{7,6},{0,7},{9,8},{10,9},{11,1... | collective-permute-start | bytes 12344 | tf_op jit(solution)/shard_map/ppermute | solution.py:24
  33.3 6.1 %collective-permute-start.6 = (f32[2,514,1]{1,0,2:T(2,128)S(1)}, f32[2,514,1]{1,0,2:T(2,128)S(1)}, u32[]{:S(2)}, u32[]{:S(2)}) collective-permute-start(f32[2,514,1]{1,0,2:T(2,128)S(1)} %copy.208), channel_id=1, source_target_pairs={{0,1},{1,2},{2,3},{3,4},{4,5},{5,6},{6,7},{7,0},{8,9},{9,10},{10,1... | collective-permute-start | bytes 12344 | tf_op jit(solution)/shard_map/ppermute | solution.py:22
  34.3 5.4 %collective-permute-start.7 = (f32[2,514,1]{1,0,2:T(2,128)S(1)}, f32[2,514,1]{1,0,2:T(2,128)S(1)}, u32[]{:S(2)}, u32[]{:S(2)}) collective-permute-start(f32[2,514,1]{1,0,2:T(2,128)S(1)} %copy.209), channel_id=1, source_target_pairs={{1,0},{2,1},{3,2},{4,3},{5,4},{6,5},{7,6},{0,7},{9,8},{10,9},{11,1... | collective-permute-start | bytes 12344 | tf_op jit(solution)/shard_map/ppermute | solution.py:24
  52.1 4.9 %collective-permute-start.8 = (f32[2,1,512]{2,1,0:T(1,128)S(1)}, f32[2,1,512]{2,1,0:T(1,128)S(1)}, u32[]{:S(2)}, u32[]{:S(2)}) collective-permute-start(f32[2,1,512]{2,1,0:T(1,128)S(1)} %get-tuple-element.86), channel_id=1, source_target_pairs={{0,8},{8,16},{16,24},{24,32},{32,40},{40,48},{48,56},{56,64},{64,7... | collective-permute-start | bytes 12296 | tf_op jit(solution)/shard_map/ppermute | solution.py:22
  53.3 3.8 %collective-permute-start.9 = (f32[2,1,512]{2,1,0:T(1,128)S(1)}, f32[2,1,512]{2,1,0:T(1,128)S(1)}, u32[]{:S(2)}, u32[]{:S(2)}) collective-permute-start(f32[2,1,512]{2,1,0:T(1,128)S(1)} %get-tuple-element.87), channel_id=1, source_target_pairs={{8,0},{16,8},{24,16},{32,24},{40,32},{48,40},{56,48},{64,56},{72,6... | collective-permute-start | bytes 12296 | tf_op jit(solution)/shard_map/ppermute | solution.py:24
  57.6 6.6 %collective-permute-start.10 = (f32[2,514,1]{1,0,2:T(2,128)S(1)}, f32[2,514,1]{1,0,2:T(2,128)S(1)}, u32[]{:S(2)}, u32[]{:S(2)}) collective-permute-start(f32[2,514,1]{1,0,2:T(2,128)S(1)} %copy.214), channel_id=1, source_target_pairs={{0,1},{1,2},{2,3},{3,4},{4,5},{5,6},{6,7},{7,0},{8,9},{9,10},{10,1... | collective-permute-start | bytes 12344 | tf_op jit(solution)/shard_map/ppermute | solution.py:22
  59.6 4.8 %collective-permute-start.11 = (f32[2,514,1]{1,0,2:T(2,128)S(1)}, f32[2,514,1]{1,0,2:T(2,128)S(1)}, u32[]{:S(2)}, u32[]{:S(2)}) collective-permute-start(f32[2,514,1]{1,0,2:T(2,128)S(1)} %copy.215), channel_id=1, source_target_pairs={{1,0},{2,1},{3,2},{4,3},{5,4},{6,5},{7,6},{0,7},{9,8},{10,9},{11,1... | collective-permute-start | bytes 12344 | tf_op jit(solution)/shard_map/ppermute | solution.py:24
  71.1 5.9 %collective-permute-start.12 = (f32[2,1,512]{2,1,0:T(1,128)S(1)}, f32[2,1,512]{2,1,0:T(1,128)S(1)}, u32[]{:S(2)}, u32[]{:S(2)}) collective-permute-start(f32[2,1,512]{2,1,0:T(1,128)S(1)} %get-tuple-element.84), channel_id=1, source_target_pairs={{0,8},{8,16},{16,24},{24,32},{32,40},{40,48},{48,56},{56,64},{64,7... | collective-permute-start | bytes 12296 | tf_op jit(solution)/shard_map/ppermute | solution.py:22
  71.8 5.4 %collective-permute-start.13 = (f32[2,1,512]{2,1,0:T(1,128)S(1)}, f32[2,1,512]{2,1,0:T(1,128)S(1)}, u32[]{:S(2)}, u32[]{:S(2)}) collective-permute-start(f32[2,1,512]{2,1,0:T(1,128)S(1)} %get-tuple-element.85), channel_id=1, source_target_pairs={{8,0},{16,8},{24,16},{32,24},{40,32},{48,40},{56,48},{64,56},{72,6... | collective-permute-start | bytes 12296 | tf_op jit(solution)/shard_map/ppermute | solution.py:24
  77.7 6.4 %collective-permute-start.14 = (f32[2,514,1]{1,0,2:T(2,128)S(1)}, f32[2,514,1]{1,0,2:T(2,128)S(1)}, u32[]{:S(2)}, u32[]{:S(2)}) collective-permute-start(f32[2,514,1]{1,0,2:T(2,128)S(1)} %copy.220), channel_id=1, source_target_pairs={{0,1},{1,2},{2,3},{3,4},{4,5},{5,6},{6,7},{7,0},{8,9},{9,10},{10,1... | collective-permute-start | bytes 12344 | tf_op jit(solution)/shard_map/ppermute | solution.py:22
  79.9 4.4 %collective-permute-start.15 = (f32[2,514,1]{1,0,2:T(2,128)S(1)}, f32[2,514,1]{1,0,2:T(2,128)S(1)}, u32[]{:S(2)}, u32[]{:S(2)}) collective-permute-start(f32[2,514,1]{1,0,2:T(2,128)S(1)} %copy.221), channel_id=1, source_target_pairs={{1,0},{2,1},{3,2},{4,3},{5,4},{6,5},{7,6},{0,7},{9,8},{10,9},{11,1... | collective-permute-start | bytes 12344 | tf_op jit(solution)/shard_map/ppermute | solution.py:24
  91.0 6.3 %collective-permute-start.16 = (f32[2,1,512]{2,1,0:T(1,128)S(1)}, f32[2,1,512]{2,1,0:T(1,128)S(1)}, u32[]{:S(2)}, u32[]{:S(2)}) collective-permute-start(f32[2,1,512]{2,1,0:T(1,128)S(1)} %get-tuple-element.82), channel_id=1, source_target_pairs={{0,8},{8,16},{16,24},{24,32},{32,40},{40,48},{48,56},{56,64},{64,7... | collective-permute-start | bytes 12296 | tf_op jit(solution)/shard_map/ppermute | solution.py:22
  91.0 6.4 %collective-permute-start.17 = (f32[2,1,512]{2,1,0:T(1,128)S(1)}, f32[2,1,512]{2,1,0:T(1,128)S(1)}, u32[]{:S(2)}, u32[]{:S(2)}) collective-permute-start(f32[2,1,512]{2,1,0:T(1,128)S(1)} %get-tuple-element.83), channel_id=1, source_target_pairs={{8,0},{16,8},{24,16},{32,24},{40,32},{48,40},{56,48},{64,56},{72,6... | collective-permute-start | bytes 12296 | tf_op jit(solution)/shard_map/ppermute | solution.py:24
  97.9 6.3 %collective-permute-start.18 = (f32[2,514,1]{1,0,2:T(2,128)S(1)}, f32[2,514,1]{1,0,2:T(2,128)S(1)}, u32[]{:S(2)}, u32[]{:S(2)}) collective-permute-start(f32[2,514,1]{1,0,2:T(2,128)S(1)} %copy.226), channel_id=1, source_target_pairs={{0,1},{1,2},{2,3},{3,4},{4,5},{5,6},{6,7},{7,0},{8,9},{9,10},{10,1... | collective-permute-start | bytes 12344 | tf_op jit(solution)/shard_map/ppermute | solution.py:22
  100.8 4.0 %collective-permute-start.19 = (f32[2,514,1]{1,0,2:T(2,128)S(1)}, f32[2,514,1]{1,0,2:T(2,128)S(1)}, u32[]{:S(2)}, u32[]{:S(2)}) collective-permute-start(f32[2,514,1]{1,0,2:T(2,128)S(1)} %copy.227), channel_id=1, source_target_pairs={{1,0},{2,1},{3,2},{4,3},{5,4},{6,5},{7,6},{0,7},{9,8},{10,9},{11,1... | collective-permute-start | bytes 12344 | tf_op jit(solution)/shard_map/ppermute | solution.py:24
  111.4 6.4 %collective-permute-start.20 = (f32[2,1,512]{2,1,0:T(1,128)S(1)}, f32[2,1,512]{2,1,0:T(1,128)S(1)}, u32[]{:S(2)}, u32[]{:S(2)}) collective-permute-start(f32[2,1,512]{2,1,0:T(1,128)S(1)} %get-tuple-element.80), channel_id=1, source_target_pairs={{0,8},{8,16},{16,24},{24,32},{32,40},{40,48},{48,56},{56,64},{64,7... | collective-permute-start | bytes 12296 | tf_op jit(solution)/shard_map/ppermute | solution.py:22
  111.5 6.6 %collective-permute-start.21 = (f32[2,1,512]{2,1,0:T(1,128)S(1)}, f32[2,1,512]{2,1,0:T(1,128)S(1)}, u32[]{:S(2)}, u32[]{:S(2)}) collective-permute-start(f32[2,1,512]{2,1,0:T(1,128)S(1)} %get-tuple-element.81), channel_id=1, source_target_pairs={{8,0},{16,8},{24,16},{32,24},{40,32},{48,40},{56,48},{64,56},{72,6... | collective-permute-start | bytes 12296 | tf_op jit(solution)/shard_map/ppermute | solution.py:24
  118.6 6.1 %collective-permute-start.22 = (f32[2,514,1]{1,0,2:T(2,128)S(1)}, f32[2,514,1]{1,0,2:T(2,128)S(1)}, u32[]{:S(2)}, u32[]{:S(2)}) collective-permute-start(f32[2,514,1]{1,0,2:T(2,128)S(1)} %copy.232), channel_id=1, source_target_pairs={{0,1},{1,2},{2,3},{3,4},{4,5},{5,6},{6,7},{7,0},{8,9},{9,10},{10,1... | collective-permute-start | bytes 12344 | tf_op jit(solution)/shard_map/ppermute | solution.py:22
  121.1 4.4 %collective-permute-start.23 = (f32[2,514,1]{1,0,2:T(2,128)S(1)}, f32[2,514,1]{1,0,2:T(2,128)S(1)}, u32[]{:S(2)}, u32[]{:S(2)}) collective-permute-start(f32[2,514,1]{1,0,2:T(2,128)S(1)} %copy.233), channel_id=1, source_target_pairs={{1,0},{2,1},{3,2},{4,3},{5,4},{6,5},{7,6},{0,7},{9,8},{10,9},{11,1... | collective-permute-start | bytes 12344 | tf_op jit(solution)/shard_map/ppermute | solution.py:24
  132.1 6.4 %collective-permute-start.24 = (f32[2,1,512]{2,1,0:T(1,128)S(1)}, f32[2,1,512]{2,1,0:T(1,128)S(1)}, u32[]{:S(2)}, u32[]{:S(2)}) collective-permute-start(f32[2,1,512]{2,1,0:T(1,128)S(1)} %get-tuple-element.78), channel_id=1, source_target_pairs={{0,8},{8,16},{16,24},{24,32},{32,40},{40,48},{48,56},{56,64},{64,7... | collective-permute-start | bytes 12296 | tf_op jit(solution)/shard_map/ppermute | solution.py:22
  132.2 6.6 %collective-permute-start.25 = (f32[2,1,512]{2,1,0:T(1,128)S(1)}, f32[2,1,512]{2,1,0:T(1,128)S(1)}, u32[]{:S(2)}, u32[]{:S(2)}) collective-permute-start(f32[2,1,512]{2,1,0:T(1,128)S(1)} %get-tuple-element.79), channel_id=1, source_target_pairs={{8,0},{16,8},{24,16},{32,24},{40,32},{48,40},{56,48},{64,56},{72,6... | collective-permute-start | bytes 12296 | tf_op jit(solution)/shard_map/ppermute | solution.py:24
  139.3 6.1 %collective-permute-start.26 = (f32[2,514,1]{1,0,2:T(2,128)S(1)}, f32[2,514,1]{1,0,2:T(2,128)S(1)}, u32[]{:S(2)}, u32[]{:S(2)}) collective-permute-start(f32[2,514,1]{1,0,2:T(2,128)S(1)} %copy.238), channel_id=1, source_target_pairs={{0,1},{1,2},{2,3},{3,4},{4,5},{5,6},{6,7},{7,0},{8,9},{9,10},{10,1... | collective-permute-start | bytes 12344 | tf_op jit(solution)/shard_map/ppermute | solution.py:22
  141.9 4.0 %collective-permute-start.27 = (f32[2,514,1]{1,0,2:T(2,128)S(1)}, f32[2,514,1]{1,0,2:T(2,128)S(1)}, u32[]{:S(2)}, u32[]{:S(2)}) collective-permute-start(f32[2,514,1]{1,0,2:T(2,128)S(1)} %copy.239), channel_id=1, source_target_pairs={{1,0},{2,1},{3,2},{4,3},{5,4},{6,5},{7,6},{0,7},{9,8},{10,9},{11,1... | collective-permute-start | bytes 12344 | tf_op jit(solution)/shard_map/ppermute | solution.py:24
  153.9 6.4 %collective-permute-start.28 = (f32[2,1,512]{2,1,0:T(1,128)S(1)}, f32[2,1,512]{2,1,0:T(1,128)S(1)}, u32[]{:S(2)}, u32[]{:S(2)}) collective-permute-start(f32[2,1,512]{2,1,0:T(1,128)S(1)} %get-tuple-element.76), channel_id=1, source_target_pairs={{0,8},{8,16},{16,24},{24,32},{32,40},{40,48},{48,56},{56,64},{64,7... | collective-permute-start | bytes 12296 | tf_op jit(solution)/shard_map/ppermute | solution.py:22
  154.0 6.6 %collective-permute-start.29 = (f32[2,1,512]{2,1,0:T(1,128)S(1)}, f32[2,1,512]{2,1,0:T(1,128)S(1)}, u32[]{:S(2)}, u32[]{:S(2)}) collective-permute-start(f32[2,1,512]{2,1,0:T(1,128)S(1)} %get-tuple-element.77), channel_id=1, source_target_pairs={{8,0},{16,8},{24,16},{32,24},{40,32},{48,40},{56,48},{64,56},{72,6... | collective-permute-start | bytes 12296 | tf_op jit(solution)/shard_map/ppermute | solution.py:24
  161.1 6.1 %collective-permute-start.30 = (f32[2,514,1]{1,0,2:T(2,128)S(1)}, f32[2,514,1]{1,0,2:T(2,128)S(1)}, u32[]{:S(2)}, u32[]{:S(2)}) collective-permute-start(f32[2,514,1]{1,0,2:T(2,128)S(1)} %copy.244), channel_id=1, source_target_pairs={{0,1},{1,2},{2,3},{3,4},{4,5},{5,6},{6,7},{7,0},{8,9},{9,10},{10,1... | collective-permute-start | bytes 12344 | tf_op jit(solution)/shard_map/ppermute | solution.py:22
  163.6 4.3 %collective-permute-start.31 = (f32[2,514,1]{1,0,2:T(2,128)S(1)}, f32[2,514,1]{1,0,2:T(2,128)S(1)}, u32[]{:S(2)}, u32[]{:S(2)}) collective-permute-start(f32[2,514,1]{1,0,2:T(2,128)S(1)} %copy.245), channel_id=1, source_target_pairs={{1,0},{2,1},{3,2},{4,3},{5,4},{6,5},{7,6},{0,7},{9,8},{10,9},{11,1... | collective-permute-start | bytes 12344 | tf_op jit(solution)/shard_map/ppermute | solution.py:24
  267.7 6.3 %collective-permute-start.32 = (f32[2,1,128]{2,1,0:T(1,128)S(1)}, f32[2,1,128]{2,1,0:T(1,128)S(1)}, u32[]{:S(2)}, u32[]{:S(2)}) collective-permute-start(f32[2,1,128]{2,1,0:T(1,128)S(1)} %get-tuple-element.112), channel_id=1, source_target_pairs={{0,8},{8,16},{16,24},{24,32},{32,40},{40,48},{48,56},{56,64},{64,7... | collective-permute-start | bytes 3080 | tf_op jit(solution)/shard_map/ppermute | solution.py:22
  267.7 6.5 %collective-permute-start.33 = (f32[2,1,128]{2,1,0:T(1,128)S(1)}, f32[2,1,128]{2,1,0:T(1,128)S(1)}, u32[]{:S(2)}, u32[]{:S(2)}) collective-permute-start(f32[2,1,128]{2,1,0:T(1,128)S(1)} %get-tuple-element.113), channel_id=1, source_target_pairs={{8,0},{16,8},{24,16},{32,24},{40,32},{48,40},{56,48},{64,56},{72,6... | collective-permute-start | bytes 3080 | tf_op jit(solution)/shard_map/ppermute | solution.py:24
  274.4 7.6 %collective-permute-start.34 = (f32[2,130,1]{2,1,0:T(8,128)S(1)}, f32[2,130,1]{2,1,0:T(8,128)S(1)}, u32[]{:S(2)}, u32[]{:S(2)}) collective-permute-start(f32[2,130,1]{2,1,0:T(8,128)S(1)} %get-tuple-element.110), channel_id=1, source_target_pairs={{0,1},{1,2},{2,3},{3,4},{4,5},{5,6},{6,7},{7,0},{8,9},{9,10},{10,1... | collective-permute-start | bytes 3128 | tf_op jit(solution)/shard_map/ppermute | solution.py:22
  278.4 5.4 %collective-permute-start.35 = (f32[2,130,1]{2,1,0:T(8,128)S(1)}, f32[2,130,1]{2,1,0:T(8,128)S(1)}, u32[]{:S(2)}, u32[]{:S(2)}) collective-permute-start(f32[2,130,1]{2,1,0:T(8,128)S(1)} %get-tuple-element.111), channel_id=1, source_target_pairs={{1,0},{2,1},{3,2},{4,3},{5,4},{6,5},{7,6},{0,7},{9,8},{10,9},{11,1... | collective-permute-start | bytes 3128 | tf_op jit(solution)/shard_map/ppermute | solution.py:24
  (25 other events, 197.4 us)
